TPU v7x, 32 devices: a whole 2x2x4 slice. The times are simulated.
32 devices in a mesh: dom: 8 (over z, y), col: 4 (over x, core).
Axes of the slice: x: 2, y: 2, z: 4, core: 2. Of those that a mesh axis runs over, the one named last changes fastest.
Arguments:
- right_side: float32 [3, 64, 32768], P(None, 'col', 'dom'), may hold values from -90 to 90, as said below
- stiffness: float32 [64, 32768], P(None, 'dom'), may hold values from -1 to 9, as said below
- contact: float32 [64, 32768], P(None, 'dom'), may hold values from -1 to 60, as said below
- pair_local: int32 [512], P('dom'), may hold values from 0 to 63
- pair_partner: int32 [512], P('dom'), may hold values from 0 to 71, as said below
- pair_count: int32 [8], P('dom'), may hold values from 16 to 64, as said below
- objective_weight: float32 [3, 32768], P(None, 'dom'), may hold values from -20 to 20
Outputs:
- solution_field: float32 [3, 64, 32768], P(None, 'col', 'dom')
- residual: float32 [3, 64, 32768], P(None, 'col', 'dom')
- param_step: float32 [64], P('col')
Inputs may be any that keep to these rules, and one draw needn't show every extreme that they name: `right_side`: varies from node to node. `stiffness`: every patch's block is symmetric and diagonally dominant with a positive diagonal. `contact`: every slot's block is symmetric and diagonally dominant with a nonnegative diagonal. `pair_partner`: A value below 64 names another patch of the slot's own partition; a value 64 + q names patch q of the next partition, with q below 8; slots of the last partition name only their own partition. `pair_count`: some partition has all 64 slots live.
All inputs are finite; a program needn't handle non-finite values.
Results may differ from a plain program's by a relative error of at most 0.0003.
Values sent between devices are 32-bit elements; how exact they have to be, the bound alone decides.
No kernel may reach another device: no remote copies, remote signals or barrier semaphores. Data moves between devices by JAX's collectives and lax.ppermute only.
A program may use at most 64 MiB of HBM per device.

v0:
```python
import jax
import jax.numpy as jnp
from jax import lax
from jax.sharding import PartitionSpec as P

PN = 64
NB = 8
COLS = 64
ITERS = 2


def shifted(value, axis, by):
    count = lax.axis_size(axis)
    pairs = [(i, i + by) for i in range(count) if 0 <= i + by < count]
    return lax.ppermute(value, axis, pairs)


def column_sums(left, right):
    return jnp.sum(left * right, axis=(0, 2))


def shards(right_side, stiffness, contact, pair_local, pair_partner, pair_count, objective_weight):
    components, columns, node_count = right_side.shape
    patches = node_count // PN
    pair_total = pair_local.shape[0]
    row_count = components * columns
    stiff_blocks = stiffness.reshape(PN, patches, PN)
    pair_blocks = contact.reshape(PN, pair_total, PN)
    live_mask = (jnp.arange(pair_total, dtype=jnp.int32) < pair_count[0]).astype(jnp.float32)
    joined_width = patches + NB
    slot_ids = jnp.arange(joined_width, dtype=jnp.int32)
    incidence = (pair_local[:, None] == slot_ids[None, :]).astype(jnp.float32) - (
        pair_partner[:, None] == slot_ids[None, :]
    ).astype(jnp.float32)

    def squares(vector):
        return lax.psum(column_sums(vector, vector), "dom")

    solution_field = jnp.zeros_like(right_side)
    residual = right_side
    direction = right_side
    norm_now = squares(residual)
    for iteration in range(ITERS):
        field_rows = direction.reshape(row_count, patches, PN)
        far_side = shifted(direction[:, :, : NB * PN], "dom", -1)
        far_rows = far_side.reshape(row_count, NB, PN)
        joined = jnp.concatenate([field_rows, far_rows], axis=1)
        gap_rows = (
            jnp.take(field_rows, pair_local, axis=1) - jnp.take(joined, pair_partner, axis=1)
        ) * live_mask[None, :, None]
        forces = jnp.einsum("cki,ikj->ckj", gap_rows, pair_blocks, precision=lax.Precision.HIGHEST)
        elastic = jnp.einsum(
            "cpi,ipj->cpj", field_rows, stiff_blocks, precision=lax.Precision.HIGHEST
        )
        spread = jnp.einsum("ckj,kw->cwj", forces, incidence, precision=lax.Precision.HIGHEST)
        own_spread = spread[:, :patches]
        received = shifted(spread[:, patches:].reshape(components, columns, NB * PN), "dom", 1)
        applied = (elastic + own_spread).reshape(components, columns, node_count)
        applied = applied.at[:, :, : NB * PN].add(received)
        step_size = norm_now / lax.psum(column_sums(direction, applied), "dom")
        solution_field = solution_field + step_size[None, :, None] * direction
        residual = residual - step_size[None, :, None] * applied
        norm_next = squares(residual)
        direction = residual + (norm_next / norm_now)[None, :, None] * direction
        norm_now = norm_next
    partial_gradient = jnp.sum(objective_weight[:, None, :] * solution_field, axis=(0, 2))
    gradient = lax.psum(partial_gradient, "dom")
    square_total = lax.psum(jnp.sum(gradient * gradient), "col")
    param_step = gradient / jnp.sqrt(square_total / COLS + 1e-06)
    return (solution_field, residual, param_step)


def solution(mesh):
    placed = (
        P(None, "col", "dom"),
        P(None, "dom"),
        P(None, "dom"),
        P("dom"),
        P("dom"),
        P("dom"),
        P(None, "dom"),
    )
    return jax.shard_map(
        shards,
        mesh=mesh,
        in_specs=placed,
        out_specs=(P(None, "col", "dom"), P(None, "col", "dom"), P("col")),
        check_vma=False,
    )
```

profile of v0, /device:TPU:0, one launch (start us, length us, event | category | flops | bytes accessed | tf_op | source)
XLA Modules:
  0.0 180.9 jit_solution(2643704245959054977)
XLA Ops:
  0.6 0.0 copy-start.9
  0.7 0.9 slice.66
  1.6 1.3 collective-permute-start
  2.9 1.8 reshape.118
  4.6 0.0 copy-done.10
  4.7 0.0 copy-start.7
  4.7 2.1 %copy.25 = f32[48,64,64]{2,0,1:T(8,128)} copy(f32[48,64,64]{2,1,0:T(8,128)S(1)} %reshape.118) | data formatting | bytes 1572864 | tf_op jit(solution)/shard_map/reshape | solution.py:44
  6.8 2.1 %reshape.120 = f32[64,64,64]{2,1,0:T(8,128)} reshape(f32[64,4096]{1,0:T(8,128)S(1)} %copy-done.7) | data formatting | bytes 2097152 | tf_op jit(solution)/shard_map/reshape | solution.py:28
  9.6 2.0 %reshape.117 = f32[64,64,64]{2,1,0:T(8,128)S(1)} reshape(f32[64,4096]{1,0:T(8,128)} %param.16) | data formatting | bytes 2097152 | tf_op jit(solution)/shard_map/reshape | solution.py:27
  11.6 4.1 %gather_fusion = f32[64,48,64]{2,1,0:T(8,128)} fusion(f32[48,64,64]{2,0,1:T(8,128)} %copy.25, s32[1024]{0:T(1024)S(1)} %pad_clamp_fusion.1), kind=kCustom, calls=%fused_computation.clone | custom fusion | bytes 1573120 | tf_op jit(solution)/shard_map/jit(_take)/gather | solution.py:49
  15.7 0.0 collective-permute-done
  15.7 0.1 reshape.119
  15.8 2.8 %pad_maximum_fusion = f32[48,72,64]{2,0,1:T(8,128)} fusion(f32[48,8,64]{2,0,1:T(8,128)S(1)} %copy.28, f32[48,64,64]{2,0,1:T(8,128)} %copy.25), kind=kLoop, calls=%fused_computation.12 | loop fusion | flops 221184 | bytes 1769472 | tf_op jit(solution)/shard_map/concatenate | solution.py:47
  18.6 3.3 %gather_fusion.1 = f32[64,48,64]{2,1,0:T(8,128)} fusion(f32[48,72,64]{2,0,1:T(8,128)} %pad_maximum_fusion, s32[1024]{0:T(1024)S(1)} %pad_clamp_fusion), kind=kCustom, calls=%fused_computation.1.clone | custom fusion | bytes 1573120 | tf_op jit(solution)/shard_map/jit(_take)/gather | solution.py:49
  21.8 7.0 %fusion.18 = f32[48,64,64]{2,0,1:T(8,128)} fusion(f32[64,64,64]{2,1,0:T(8,128)} %reshape.120, f32[64,48,64]{2,1,0:T(8,128)} %gather_fusion.1, f32[64,48,64]{2,1,0:T(8,128)} %gather_fusion, f32[64]{0:T(128)S(1)} %compare_convert_fusion, pred[64]{0:T(512)(128)(4,1)S(1)} %get-tuple-element.36, pred[64]{0:T(512)(128)(4,1)S(1)} %get-tuple-element.37), kind=kOutput, calls=%fused_computation.26 | convolution fusion | flops 151781376 | bytes 3408256 | tf_op jit(solution)/shard_map/cki,ikj->ckj/dot_general | solution.py:51
  28.9 3.2 %copy.30 = f32[48,64,64]{1,2,0:T(8,128)} copy(f32[48,64,64]{2,0,1:T(8,128)} %fusion.18) | data formatting | bytes 1572864 | tf_op jit(solution)/shard_map/cki,ikj->ckj/transpose | solution.py:51
  32.1 4.0 %fusion.43 = f32[72,3072]{0,1} fusion(f32[64,3072]{0,1:T(8,128)} %bitcast.54, s32[64]{0:T(128)S(1)} %copy-done.9, s32[64]{0:T(128)S(1)} %copy-done.10), kind=kOutput, calls=%fused_computation.52 | convolution fusion | flops 169892352 | bytes 1671680
  36.1 2.7 %copy.31 = f32[72,48,64]{2,1,0:T(8,128)} copy(f32[72,48,64]{0,2,1:T(8,128)} %bitcast.55) | data formatting | bytes 1769472 | tf_op jit(solution)/shard_map/ckj,kw->cwj/dot_general | solution.py:55
  38.9 0.9 slice.84
  39.8 0.1 copy.33
  39.9 0.1 reshape.122
  40.0 5.7 %collective-permute-start.1 = (f32[3,16,512]{2,1,0:T(8,128)S(1)}, f32[3,16,512]{2,1,0:T(8,128)S(1)}, u32[]{:S(2)}, u32[]{:S(2)}) collective-permute-start(f32[3,16,512]{2,1,0:T(8,128)S(1)} %reshape.122), channel_id=1, source_target_pairs={{0,4},{4,8},{8,12},{12,16},{16,20},{20,24},{24,28},{1,5},{5,9},{9,... | collective-permute-start | bytes 294920 | tf_op jit(solution)/shard_map/ppermute | solution.py:15
  45.7 6.0 %slice_add_fusion.1 = f32[48,64,64]{2,0,1:T(8,128)S(1)} fusion(f32[48,72,64]{2,0,1:T(8,128)} %bitcast.53, f32[64,64,64]{2,1,0:T(8,128)S(1)} %reshape.117, f32[48,64,64]{2,1,0:T(8,128)} %copy-done.2), kind=kOutput, calls=%fused_computation.15 | convolution fusion | flops 151191552 | bytes 3407872 | tf_op jit(solution)/shard_map/cpi,ipj->cpj/dot_general | solution.py:52
  51.6 0.5 copy.32
  52.2 0.0 copy-start
  52.2 0.5 reshape.121
  52.7 0.0 collective-permute-done.1
  52.7 0.6 copy-done
  53.3 0.3 multiply_reduce_fusion.3
  53.6 20.3 %all-reduce = (f32[16]{0:T(128)S(1)}, f32[16]{0:T(128)S(1)}) all-reduce(f32[16]{0:T(128)S(1)} %get-tuple-element.30, f32[16]{0:T(128)S(1)} %get-tuple-element.29), channel_id=1, replica_groups=mesh['dom'=8,'col'=4] {'dom'}, use_global_device_ids=true, to_apply=%region_1.0 | all-reduce | flops 32 | bytes 256 | tf_op jit(solution)/shard_map/psum | solution.py:37
  73.8 0.3 multiply_reduce_fusion.2
  74.2 17.1 %psum.44 = f32[16]{0:T(128)S(1)} all-reduce(f32[16]{0:T(128)S(1)} %multiply_reduce_fusion.2), channel_id=1, replica_groups=mesh['dom'=8,'col'=4] {'dom'}, use_global_device_ids=true, to_apply=%region_5.8 | all-reduce | flops 16 | bytes 128 | tf_op jit(solution)/shard_map/psum | solution.py:37
  91.3 0.2 multiply_add_fusion.1
  91.5 0.0 copy-start.4
  91.5 1.5 collective-permute-start.2
  93.0 0.0 copy-done.4
  93.1 1.8 reshape.123
  94.9 2.3 %copy.34 = f32[48,64,64]{2,0,1:T(8,128)S(1)} copy(f32[48,64,64]{2,1,0:T(8,128)} %reshape.123) | data formatting | bytes 1572864 | tf_op jit(solution)/shard_map/reshape | solution.py:44
  97.2 1.8 %gather_fusion.2 = f32[64,48,64]{2,1,0:T(8,128)} fusion(f32[48,64,64]{2,0,1:T(8,128)S(1)} %copy.34, s32[1024]{0:T(1024)S(1)} %pad_clamp_fusion.1), kind=kCustom, calls=%fused_computation.2.clone | custom fusion | bytes 1573120 | tf_op jit(solution)/shard_map/jit(_take)/gather | solution.py:49
  99.0 0.0 collective-permute-done.2
  99.0 0.1 reshape.124
  99.1 1.3 pad_maximum_fusion.1
  100.5 3.5 %gather_fusion.3 = f32[64,48,64]{2,1,0:T(8,128)} fusion(f32[48,72,64]{2,0,1:T(8,128)} %pad_maximum_fusion.1, s32[1024]{0:T(1024)S(1)} %pad_clamp_fusion), kind=kCustom, calls=%fused_computation.3.clone | custom fusion | bytes 1573120 | tf_op jit(solution)/shard_map/jit(_take)/gather | solution.py:49
  104.0 0.0 copy-done.6
  104.0 6.6 %fusion.23 = f32[48,64,64]{2,0,1:T(8,128)} fusion(f32[64,64,64]{2,1,0:T(8,128)} %reshape.120, f32[64,48,64]{2,1,0:T(8,128)} %gather_fusion.3, f32[64,48,64]{2,1,0:T(8,128)S(1)} %copy-done.6, f32[64]{0:T(128)S(1)} %compare_convert_fusion, pred[64]{0:T(512)(128)(4,1)S(1)} %get-tuple-element.36, pred[64]{0:T(512)(128)(4,1)S(1)} %get-tuple-element.37), kind=kOutput, calls=%fused_computation.27 | convolution fusion | flops 151781376 | bytes 3408256 | tf_op jit(solution)/shard_map/cki,ikj->ckj/dot_general | solution.py:51
  110.5 2.0 %copy.40 = f32[48,64,64]{1,2,0:T(8,128)S(1)} copy(f32[48,64,64]{2,0,1:T(8,128)} %fusion.23) | data formatting | bytes 1572864 | tf_op jit(solution)/shard_map/cki,ikj->ckj/transpose | solution.py:51
  112.5 2.6 %fusion.42 = f32[72,3072]{0,1} fusion(f32[64,3072]{0,1:T(8,128)S(1)} %bitcast.56, s32[64]{0:T(128)S(1)} %copy-done.9, s32[64]{0:T(128)S(1)} %copy-done.10), kind=kOutput, calls=%fused_computation.51 | convolution fusion | flops 169892352 | bytes 1671680
  115.1 2.9 %copy.41 = f32[72,48,64]{2,1,0:T(8,128)} copy(f32[72,48,64]{0,2,1:T(8,128)} %bitcast.57) | data formatting | bytes 1769472 | tf_op jit(solution)/shard_map/ckj,kw->cwj/dot_general | solution.py:55
  118.0 0.9 slice.88
  118.9 0.1 copy.43
  119.0 0.1 reshape.126
  119.1 4.9 %collective-permute-start.3 = (f32[3,16,512]{2,1,0:T(8,128)S(1)}, f32[3,16,512]{2,1,0:T(8,128)S(1)}, u32[]{:S(2)}, u32[]{:S(2)}) collective-permute-start(f32[3,16,512]{2,1,0:T(8,128)S(1)} %reshape.126), channel_id=1, source_target_pairs={{0,4},{4,8},{8,12},{12,16},{16,20},{20,24},{24,28},{1,5},{5,9},{9,... | collective-permute-start | bytes 294920 | tf_op jit(solution)/shard_map/ppermute | solution.py:15
  124.0 6.2 %slice_add_fusion = f32[48,64,64]{2,0,1:T(8,128)S(1)} fusion(f32[48,72,64]{2,0,1:T(8,128)} %bitcast.51, f32[64,64,64]{2,1,0:T(8,128)} %copy-done.1, f32[48,64,64]{2,1,0:T(8,128)S(1)} %copy-done.3), kind=kOutput, calls=%fused_computation.14 | convolution fusion | flops 151191552 | bytes 3407872 | tf_op jit(solution)/shard_map/cpi,ipj->cpj/dot_general | solution.py:52
  130.2 1.6 copy.42
  131.8 2.0 %reshape.125 = f32[3,16,4096]{2,1,0:T(8,128)S(1)} reshape(f32[48,64,64]{2,1,0:T(8,128)} %copy.42) | data formatting | bytes 1572864 | tf_op jit(solution)/shard_map/reshape | solution.py:58
  133.8 0.0 collective-permute-done.3
  133.9 0.2 multiply_reduce_fusion.1
  134.1 20.0 %psum.45 = f32[16]{0:T(128)S(1)} all-reduce(f32[16]{0:T(128)S(1)} %multiply_reduce_fusion.1), channel_id=1, replica_groups=mesh['dom'=8,'col'=4] {'dom'}, use_global_device_ids=true, to_apply=%region_7.10 | all-reduce | flops 16 | bytes 128 | tf_op jit(solution)/shard_map/psum | solution.py:60
  154.1 0.0 copy-done.8
  154.2 1.6 multiply_reduce_fusion
  155.7 17.1 %psum.46 = f32[16]{0:T(128)S(1)} all-reduce(f32[16]{0:T(128)S(1)} %get-tuple-element.33), channel_id=1, replica_groups=mesh['dom'=8,'col'=4] {'dom'}, use_global_device_ids=true, to_apply=%region_9.12 | all-reduce | flops 16 | bytes 128 | tf_op jit(solution)/shard_map/psum | solution.py:67
  172.8 0.6 multiply_reduce_fusion.5
  173.5 6.3 %psum.47 = f32[]{:T(128)} all-reduce(f32[]{:T(128)} %multiply_reduce_fusion.5), channel_id=1, replica_groups=mesh['dom'=8,'col'=4] {'col'}, use_global_device_ids=true, to_apply=%region_11.14 | all-reduce | flops 1 | bytes 8 | tf_op jit(solution)/shard_map/psum | solution.py:68
  180.4 0.5 broadcast_divide_fusion
  (27 shorter events, 0.2 us)
Async XLA Ops:
  0.6 4.0 %copy-start.9 = (s32[64]{0:T(128)S(1)}, s32[64]{0:T(128)}, u32[]{:S(2)}) copy-start(s32[64]{0:T(128)} %param.19) | copy-start | bytes 772
  0.6 4.0 %copy-start.10 = (s32[64]{0:T(128)S(1)}, s32[64]{0:T(128)}, u32[]{:S(2)}) copy-start(s32[64]{0:T(128)} %param.18) | copy-start | bytes 772
  1.6 14.1 %collective-permute-start = (f32[3,16,512]{2,1,0:T(8,128)S(1)}, f32[3,16,512]{2,1,0:T(8,128)S(1)}, u32[]{:S(2)}, u32[]{:S(2)}) collective-permute-start(f32[3,16,512]{2,1,0:T(8,128)S(1)} %slice.66), channel_id=1, source_target_pairs={{4,0},{8,4},{12,8},{16,12},{20,16},{24,20},{28,24},{5,1},{9,5},{13... | collective-permute-start | bytes 294920 | tf_op jit(solution)/shard_map/ppermute | solution.py:15
  4.6 2.1 %copy-start.2 = (f32[48,64,64]{2,1,0:T(8,128)}, f32[48,64,64]{2,1,0:T(8,128)S(1)}, u32[]{:S(2)}) copy-start(f32[48,64,64]{2,1,0:T(8,128)S(1)} %reshape.118) | copy-start | bytes 2359300
  4.7 2.1 %copy-start.7 = (f32[64,4096]{1,0:T(8,128)S(1)}, f32[64,4096]{1,0:T(8,128)}, u32[]{:S(2)}) copy-start(f32[64,4096]{1,0:T(8,128)} %param.17) | copy-start | bytes 3145732
  11.6 34.1 %copy-start.1 = (f32[64,64,64]{2,1,0:T(8,128)}, f32[64,64,64]{2,1,0:T(8,128)S(1)}, u32[]{:S(2)}) copy-start(f32[64,64,64]{2,1,0:T(8,128)S(1)} %reshape.117) | copy-start | bytes 3145732
  40.0 12.7 %collective-permute-start.1 = (f32[3,16,512]{2,1,0:T(8,128)S(1)}, f32[3,16,512]{2,1,0:T(8,128)S(1)}, u32[]{:S(2)}, u32[]{:S(2)}) collective-permute-start(f32[3,16,512]{2,1,0:T(8,128)S(1)} %reshape.122), channel_id=1, source_target_pairs={{0,4},{4,8},{8,12},{12,16},{16,20},{20,24},{24,28},{1,5},{5,9},{9,... | collective-permute-start | bytes 294920 | tf_op jit(solution)/shard_map/ppermute | solution.py:15
  52.2 1.1 copy-start
  91.5 1.6 copy-start.4
  91.5 7.5 %collective-permute-start.2 = (f32[3,16,512]{2,1,0:T(8,128)S(1)}, f32[3,16,512]{2,1,0:T(8,128)S(1)}, u32[]{:S(2)}, u32[]{:S(2)}) collective-permute-start(f32[3,16,512]{2,1,0:T(8,128)S(1)} %slice.85), channel_id=1, source_target_pairs={{4,0},{8,4},{12,8},{16,12},{20,16},{24,20},{28,24},{5,1},{9,5},{13... | collective-permute-start | bytes 294920 | tf_op jit(solution)/shard_map/ppermute | solution.py:15
  100.5 3.5 %copy-start.6 = (f32[64,48,64]{2,1,0:T(8,128)S(1)}, f32[64,48,64]{2,1,0:T(8,128)}, u32[]{:S(2)}) copy-start(f32[64,48,64]{2,1,0:T(8,128)} %gather_fusion.2) | copy-start | bytes 2359300
  115.1 8.9 %copy-start.3 = (f32[48,64,64]{2,1,0:T(8,128)S(1)}, f32[48,64,64]{2,1,0:T(8,128)}, u32[]{:S(2)}) copy-start(f32[48,64,64]{2,1,0:T(8,128)} %reshape.123) | copy-start | bytes 2359300
  119.1 14.7 %collective-permute-start.3 = (f32[3,16,512]{2,1,0:T(8,128)S(1)}, f32[3,16,512]{2,1,0:T(8,128)S(1)}, u32[]{:S(2)}, u32[]{:S(2)}) collective-permute-start(f32[3,16,512]{2,1,0:T(8,128)S(1)} %reshape.126), channel_id=1, source_target_pairs={{0,4},{4,8},{8,12},{12,16},{16,20},{20,24},{24,28},{1,5},{5,9},{9,... | collective-permute-start | bytes 294920 | tf_op jit(solution)/shard_map/ppermute | solution.py:15
  131.8 2.0 %copy-start.5 = (f32[3,16,4096]{2,1,0:T(8,128)S(1)}, f32[3,16,4096]{2,1,0:T(8,128)}, u32[]{:S(2)}) copy-start(f32[3,16,4096]{2,1,0:T(8,128)} %copy-done.4) | copy-start | bytes 2359300
  131.8 22.3 %copy-start.8 = (f32[3,4096]{1,0:T(4,128)S(1)}, f32[3,4096]{1,0:T(4,128)}, u32[]{:S(2)}) copy-start(f32[3,4096]{1,0:T(4,128)} %param.21) | copy-start | bytes 147460
where the time goes:
time: 182 us; the launch traced here: 181 us
  blocking collectives  80.8 us (44%)
  local copies, waits for them, and re-layouts  44.2 us (24%)
  matrix products  32.3 us (18%)
  starting transfers between devices  13.4 us (7%)
  other arithmetic  7.92 us (4%)
  between operations  2.3 us (1%)
    psum x2, blocking collectives, squares(): return lax.psum(column_sums(vector, vector), 'dom')  37.4 us
    psum x1, blocking collectives, shards(): step_size = norm_now / lax.psum(column_sums(direction, applied), 'dom')  20 us
    psum x1, blocking collectives, shards(): gradient = lax.psum(partial_gradient, 'dom')  17.1 us
    dot_general x2, matrix products, shards(): jnp.einsum('cki,ikj->ckj', gap_rows, pair_blocks, precision=lax.Precision...  13.6 us
    ppermute x4, starting transfers between devices, shifted(): return lax.ppermute(value, axis, pairs)  13.4 us
    dot_general x2, matrix products, shards(): jnp.einsum('cpi,ipj->cpj', field_rows, stiff_blocks, precision=lax.Precis...  12.1 us
    reshape x4, local copies, waits for them, and re-layouts, shards(): field_rows = direction.reshape(row_count, patches, PN)  7.94 us
    gather x2, local copies, waits for them, and re-layouts, shards(): jnp.take(joined, pair_partner, axis=1)  6.76 us
  transfers between devices with their start and end apart: 4, of which 0 were waited for; matrix products, arithmetic and copies ran while one was open for 19% of the time, Pallas kernels for 0%

commit v1 on v0

--- a/solution.py
+++ b/solution.py
@@ -34,7 +34,7 @@
     ).astype(jnp.float32)
 
     def squares(vector):
-        return lax.psum(column_sums(vector, vector), "dom")
+        return jnp.sum(lax.all_gather(column_sums(vector, vector), "dom"), axis=0)
 
     solution_field = jnp.zeros_like(right_side)
     residual = right_side

time: 182 us -> 184 us (1.011)
    psum x2 -> x0, blocking collectives: 37.4 us -> none  [squares(): return lax.psum(column_sums(vector, vector), 'dom')]
    unnamed x0 -> x2, blocking collectives: none -> 37.4 us
where the time goes in v1:
time: 184 us; the launch traced here: 183 us
  blocking collectives  80.8 us (44%)
  local copies, waits for them, and re-layouts  45.4 us (25%)
  matrix products  32.3 us (18%)
  starting transfers between devices  13.4 us (7%)
  other arithmetic  7.97 us (4%)
  between operations  3 us (2%)
    unnamed x2, blocking collectives  37.4 us
    psum x1, blocking collectives, shards(): step_size = norm_now / lax.psum(column_sums(direction, applied), 'dom')  20 us
    psum x1, blocking collectives, shards(): gradient = lax.psum(partial_gradient, 'dom')  17.1 us
    dot_general x2, matrix products, shards(): jnp.einsum('cki,ikj->ckj', gap_rows, pair_blocks, precision=lax.Precision...  13.6 us
    ppermute x4, starting transfers between devices, shifted(): return lax.ppermute(value, axis, pairs)  13.4 us
    dot_general x2, matrix products, shards(): jnp.einsum('cpi,ipj->cpj', field_rows, stiff_blocks, precision=lax.Precis...  12.1 us
    reshape x4, local copies, waits for them, and re-layouts, shards(): field_rows = direction.reshape(row_count, patches, PN)  7.94 us
    gather x2, local copies, waits for them, and re-layouts, shards(): jnp.take(joined, pair_partner, axis=1)  6.76 us
  transfers between devices with their start and end apart: 4, of which 0 were waited for; matrix products, arithmetic and copies ran while one was open for 19% of the time, Pallas kernels for 0%

profile of v1, /device:TPU:0, one launch (start us, length us, event | category | flops | bytes accessed | tf_op | source)
XLA Modules:
  0.0 182.9 jit_solution(11374105534702010633)
XLA Ops:
  0.7 0.9 slice.66
  1.6 1.3 collective-permute-start
  2.9 1.8 reshape.122
  4.7 0.0 copy-start.7
  4.7 2.1 %copy.25 = f32[48,64,64]{2,0,1:T(8,128)} copy(f32[48,64,64]{2,1,0:T(8,128)S(1)} %reshape.122) | data formatting | bytes 1572864 | tf_op jit(solution)/shard_map/reshape | solution.py:44
  6.8 2.1 %reshape.124 = f32[64,64,64]{2,1,0:T(8,128)} reshape(f32[64,4096]{1,0:T(8,128)S(1)} %copy-done.7) | data formatting | bytes 2097152 | tf_op jit(solution)/shard_map/reshape | solution.py:28
  9.6 2.0 %reshape.121 = f32[64,64,64]{2,1,0:T(8,128)S(1)} reshape(f32[64,4096]{1,0:T(8,128)} %param.16) | data formatting | bytes 2097152 | tf_op jit(solution)/shard_map/reshape | solution.py:27
  11.6 0.0 copy-start.11
  11.6 4.1 %gather_fusion = f32[64,48,64]{2,1,0:T(8,128)} fusion(f32[48,64,64]{2,0,1:T(8,128)} %copy.25, s32[1024]{0:T(1024)S(1)} %pad_clamp_fusion.1), kind=kCustom, calls=%fused_computation.clone | custom fusion | bytes 1573120 | tf_op jit(solution)/shard_map/jit(_take)/gather | solution.py:49
  15.7 0.6 dynamic-slice.16
  16.9 0.0 collective-permute-done
  16.9 0.1 reshape.123
  17.1 2.8 %pad_maximum_fusion = f32[48,72,64]{2,0,1:T(8,128)} fusion(f32[48,8,64]{2,0,1:T(8,128)S(1)} %copy.28, f32[48,64,64]{2,0,1:T(8,128)} %copy.25), kind=kLoop, calls=%fused_computation.12 | loop fusion | flops 221184 | bytes 1769472 | tf_op jit(solution)/shard_map/concatenate | solution.py:47
  19.8 3.3 %gather_fusion.1 = f32[64,48,64]{2,1,0:T(8,128)} fusion(f32[48,72,64]{2,0,1:T(8,128)} %pad_maximum_fusion, s32[1024]{0:T(1024)S(1)} %pad_clamp_fusion), kind=kCustom, calls=%fused_computation.1.clone | custom fusion | bytes 1573120 | tf_op jit(solution)/shard_map/jit(_take)/gather | solution.py:49
  23.1 7.0 %fusion.18 = f32[48,64,64]{2,0,1:T(8,128)} fusion(f32[64,64,64]{2,1,0:T(8,128)} %reshape.124, f32[64,48,64]{2,1,0:T(8,128)} %gather_fusion.1, f32[64,48,64]{2,1,0:T(8,128)} %gather_fusion, f32[64]{0:T(128)S(1)} %compare_convert_fusion, pred[64]{0:T(512)(128)(4,1)S(1)} %get-tuple-element.36, pred[64]{0:T(512)(128)(4,1)S(1)} %get-tuple-element.37), kind=kOutput, calls=%fused_computation.26 | convolution fusion | flops 151781376 | bytes 3408256 | tf_op jit(solution)/shard_map/cki,ikj->ckj/dot_general | solution.py:51
  30.2 3.2 %copy.30 = f32[48,64,64]{1,2,0:T(8,128)} copy(f32[48,64,64]{2,0,1:T(8,128)} %fusion.18) | data formatting | bytes 1572864 | tf_op jit(solution)/shard_map/cki,ikj->ckj/transpose | solution.py:51
  33.4 4.0 %fusion.43 = f32[72,3072]{0,1} fusion(f32[64,3072]{0,1:T(8,128)} %bitcast.55, s32[64]{0:T(128)S(1)} %copy-done.9, s32[64]{0:T(128)S(1)} %copy-done.10), kind=kOutput, calls=%fused_computation.52 | convolution fusion | flops 169892352 | bytes 1671680
  37.4 2.7 %copy.31 = f32[72,48,64]{2,1,0:T(8,128)} copy(f32[72,48,64]{0,2,1:T(8,128)} %bitcast.56) | data formatting | bytes 1769472 | tf_op jit(solution)/shard_map/ckj,kw->cwj/dot_general | solution.py:55
  40.1 0.9 slice.84
  41.1 0.1 copy.33
  41.2 0.1 reshape.126
  41.3 5.7 %collective-permute-start.1 = (f32[3,16,512]{2,1,0:T(8,128)S(1)}, f32[3,16,512]{2,1,0:T(8,128)S(1)}, u32[]{:S(2)}, u32[]{:S(2)}) collective-permute-start(f32[3,16,512]{2,1,0:T(8,128)S(1)} %reshape.126), channel_id=1, source_target_pairs={{0,4},{4,8},{8,12},{12,16},{16,20},{20,24},{24,28},{1,5},{5,9},{9,... | collective-permute-start | bytes 294920 | tf_op jit(solution)/shard_map/ppermute | solution.py:15
  47.0 6.0 %slice_add_fusion.1 = f32[48,64,64]{2,0,1:T(8,128)S(1)} fusion(f32[48,72,64]{2,0,1:T(8,128)} %bitcast.54, f32[64,64,64]{2,1,0:T(8,128)S(1)} %reshape.121, f32[48,64,64]{2,1,0:T(8,128)} %copy-done.2), kind=kOutput, calls=%fused_computation.15 | convolution fusion | flops 151191552 | bytes 3407872 | tf_op jit(solution)/shard_map/cpi,ipj->cpj/dot_general | solution.py:52
  52.9 0.5 copy.32
  53.4 0.0 copy-start
  53.4 0.5 reshape.125
  54.0 0.0 collective-permute-done.1
  54.0 0.6 copy-done
  54.6 0.3 multiply_reduce_fusion.3
  54.9 0.2 dynamic-update-slice.6
  55.1 20.2 %all-reduce.2 = (f32[128]{0:T(128)S(1)}, f32[16]{0:T(128)S(1)}) all-reduce(f32[128]{0:T(128)S(1)} %dynamic-update-slice.6, f32[16]{0:T(128)S(1)} %get-tuple-element.29), channel_id=2, replica_groups=mesh['dom'=8,'col'=4] {'dom'}, use_global_device_ids=true, to_apply=%add | all-reduce | flops 144 | bytes 1152
  75.3 0.1 reshape.163
  75.4 0.3 multiply_reduce_fusion.2
  75.8 0.2 dynamic-update-slice.7
  76.0 17.1 %all-reduce.1 = f32[128]{0:T(128)S(1)} all-reduce(f32[128]{0:T(128)S(1)} %dynamic-update-slice.7), channel_id=3, replica_groups=mesh['dom'=8,'col'=4] {'dom'}, use_global_device_ids=true, to_apply=%add.1 | all-reduce | flops 128 | bytes 1024
  93.2 0.1 reshape.164
  93.3 0.2 multiply_add_fusion.1
  93.5 0.0 copy-start.4
  93.5 1.5 collective-permute-start.2
  95.0 1.8 reshape.127
  96.8 2.3 %copy.34 = f32[48,64,64]{2,0,1:T(8,128)S(1)} copy(f32[48,64,64]{2,1,0:T(8,128)} %reshape.127) | data formatting | bytes 1572864 | tf_op jit(solution)/shard_map/reshape | solution.py:44
  99.1 1.8 gather_fusion.2
  100.9 0.0 collective-permute-done.2
  101.0 0.1 reshape.128
  101.1 1.3 pad_maximum_fusion.1
  102.4 3.5 %gather_fusion.3 = f32[64,48,64]{2,1,0:T(8,128)} fusion(f32[48,72,64]{2,0,1:T(8,128)} %pad_maximum_fusion.1, s32[1024]{0:T(1024)S(1)} %pad_clamp_fusion), kind=kCustom, calls=%fused_computation.3.clone | custom fusion | bytes 1573120 | tf_op jit(solution)/shard_map/jit(_take)/gather | solution.py:49
  105.9 6.6 %fusion.23 = f32[48,64,64]{2,0,1:T(8,128)} fusion(f32[64,64,64]{2,1,0:T(8,128)} %reshape.124, f32[64,48,64]{2,1,0:T(8,128)} %gather_fusion.3, f32[64,48,64]{2,1,0:T(8,128)S(1)} %copy-done.6, f32[64]{0:T(128)S(1)} %compare_convert_fusion, pred[64]{0:T(512)(128)(4,1)S(1)} %get-tuple-element.36, pred[64]{0:T(512)(128)(4,1)S(1)} %get-tuple-element.37), kind=kOutput, calls=%fused_computation.27 | convolution fusion | flops 151781376 | bytes 3408256 | tf_op jit(solution)/shard_map/cki,ikj->ckj/dot_general | solution.py:51
  112.5 2.0 %copy.40 = f32[48,64,64]{1,2,0:T(8,128)S(1)} copy(f32[48,64,64]{2,0,1:T(8,128)} %fusion.23) | data formatting | bytes 1572864 | tf_op jit(solution)/shard_map/cki,ikj->ckj/transpose | solution.py:51
  114.5 2.6 %fusion.42 = f32[72,3072]{0,1} fusion(f32[64,3072]{0,1:T(8,128)S(1)} %bitcast.57, s32[64]{0:T(128)S(1)} %copy-done.9, s32[64]{0:T(128)S(1)} %copy-done.10), kind=kOutput, calls=%fused_computation.51 | convolution fusion | flops 169892352 | bytes 1671680
  117.1 2.9 %copy.41 = f32[72,48,64]{2,1,0:T(8,128)} copy(f32[72,48,64]{0,2,1:T(8,128)} %bitcast.58) | data formatting | bytes 1769472 | tf_op jit(solution)/shard_map/ckj,kw->cwj/dot_general | solution.py:55
  120.0 0.9 slice.88
  120.9 0.1 copy.43
  121.0 0.1 reshape.130
  121.1 4.9 %collective-permute-start.3 = (f32[3,16,512]{2,1,0:T(8,128)S(1)}, f32[3,16,512]{2,1,0:T(8,128)S(1)}, u32[]{:S(2)}, u32[]{:S(2)}) collective-permute-start(f32[3,16,512]{2,1,0:T(8,128)S(1)} %reshape.130), channel_id=1, source_target_pairs={{0,4},{4,8},{8,12},{12,16},{16,20},{20,24},{24,28},{1,5},{5,9},{9,... | collective-permute-start | bytes 294920 | tf_op jit(solution)/shard_map/ppermute | solution.py:15
  126.0 6.2 %slice_add_fusion = f32[48,64,64]{2,0,1:T(8,128)S(1)} fusion(f32[48,72,64]{2,0,1:T(8,128)} %bitcast.52, f32[64,64,64]{2,1,0:T(8,128)} %copy-done.1, f32[48,64,64]{2,1,0:T(8,128)S(1)} %copy-done.3), kind=kOutput, calls=%fused_computation.14 | convolution fusion | flops 151191552 | bytes 3407872 | tf_op jit(solution)/shard_map/cpi,ipj->cpj/dot_general | solution.py:52
  132.2 1.6 copy.42
  133.8 2.0 %reshape.129 = f32[3,16,4096]{2,1,0:T(8,128)S(1)} reshape(f32[48,64,64]{2,1,0:T(8,128)} %copy.42) | data formatting | bytes 1572864 | tf_op jit(solution)/shard_map/reshape | solution.py:58
  135.8 0.2 multiply_reduce_fusion.1
  136.1 20.0 %psum.29 = f32[16]{0:T(128)S(1)} all-reduce(f32[16]{0:T(128)S(1)} %multiply_reduce_fusion.1), channel_id=1, replica_groups=mesh['dom'=8,'col'=4] {'dom'}, use_global_device_ids=true, to_apply=%region_7.10 | all-reduce | flops 16 | bytes 128 | tf_op jit(solution)/shard_map/psum | solution.py:60
  156.1 1.6 multiply_reduce_fusion
  157.7 17.1 %psum.30 = f32[16]{0:T(128)S(1)} all-reduce(f32[16]{0:T(128)S(1)} %get-tuple-element.33), channel_id=1, replica_groups=mesh['dom'=8,'col'=4] {'dom'}, use_global_device_ids=true, to_apply=%region_9.12 | all-reduce | flops 16 | bytes 128 | tf_op jit(solution)/shard_map/psum | solution.py:67
  174.8 0.6 multiply_reduce_fusion.5
  175.4 6.3 %psum.31 = f32[]{:T(128)} all-reduce(f32[]{:T(128)} %multiply_reduce_fusion.5), channel_id=1, replica_groups=mesh['dom'=8,'col'=4] {'col'}, use_global_device_ids=true, to_apply=%region_11.14 | all-reduce | flops 1 | bytes 8 | tf_op jit(solution)/shard_map/psum | solution.py:68
  182.4 0.5 broadcast_divide_fusion
  (38 shorter events, 0.3 us)
Async XLA Ops:
  0.6 4.0 %copy-start.9 = (s32[64]{0:T(128)S(1)}, s32[64]{0:T(128)}, u32[]{:S(2)}) copy-start(s32[64]{0:T(128)} %param.19) | copy-start | bytes 772
  0.6 4.0 %copy-start.10 = (s32[64]{0:T(128)S(1)}, s32[64]{0:T(128)}, u32[]{:S(2)}) copy-start(s32[64]{0:T(128)} %param.18) | copy-start | bytes 772
  1.6 15.4 %collective-permute-start = (f32[3,16,512]{2,1,0:T(8,128)S(1)}, f32[3,16,512]{2,1,0:T(8,128)S(1)}, u32[]{:S(2)}, u32[]{:S(2)}) collective-permute-start(f32[3,16,512]{2,1,0:T(8,128)S(1)} %slice.66), channel_id=1, source_target_pairs={{4,0},{8,4},{12,8},{16,12},{20,16},{24,20},{28,24},{5,1},{9,5},{13... | collective-permute-start | bytes 294920 | tf_op jit(solution)/shard_map/ppermute | solution.py:15
  4.6 2.1 %copy-start.2 = (f32[48,64,64]{2,1,0:T(8,128)}, f32[48,64,64]{2,1,0:T(8,128)S(1)}, u32[]{:S(2)}) copy-start(f32[48,64,64]{2,1,0:T(8,128)S(1)} %reshape.122) | copy-start | bytes 2359300
  4.7 2.1 %copy-start.7 = (f32[64,4096]{1,0:T(8,128)S(1)}, f32[64,4096]{1,0:T(8,128)}, u32[]{:S(2)}) copy-start(f32[64,4096]{1,0:T(8,128)} %param.17) | copy-start | bytes 3145732
  11.6 35.3 %copy-start.1 = (f32[64,64,64]{2,1,0:T(8,128)}, f32[64,64,64]{2,1,0:T(8,128)S(1)}, u32[]{:S(2)}) copy-start(f32[64,64,64]{2,1,0:T(8,128)S(1)} %reshape.121) | copy-start | bytes 3145732
  11.6 4.1 %copy-start.11 = (u32[32]{0:T(128)S(1)}, u32[32]{0:T(128)}, u32[]{:S(2)}) copy-start(u32[32]{0:T(128)} %constant.77) | copy-start | bytes 388
  41.3 12.7 %collective-permute-start.1 = (f32[3,16,512]{2,1,0:T(8,128)S(1)}, f32[3,16,512]{2,1,0:T(8,128)S(1)}, u32[]{:S(2)}, u32[]{:S(2)}) collective-permute-start(f32[3,16,512]{2,1,0:T(8,128)S(1)} %reshape.126), channel_id=1, source_target_pairs={{0,4},{4,8},{8,12},{12,16},{16,20},{20,24},{24,28},{1,5},{5,9},{9,... | collective-permute-start | bytes 294920 | tf_op jit(solution)/shard_map/ppermute | solution.py:15
  53.4 1.1 copy-start
  93.5 1.6 copy-start.4
  93.5 7.5 %collective-permute-start.2 = (f32[3,16,512]{2,1,0:T(8,128)S(1)}, f32[3,16,512]{2,1,0:T(8,128)S(1)}, u32[]{:S(2)}, u32[]{:S(2)}) collective-permute-start(f32[3,16,512]{2,1,0:T(8,128)S(1)} %slice.85), channel_id=1, source_target_pairs={{4,0},{8,4},{12,8},{16,12},{20,16},{24,20},{28,24},{5,1},{9,5},{13... | collective-permute-start | bytes 294920 | tf_op jit(solution)/shard_map/ppermute | solution.py:15
  102.4 3.5 %copy-start.6 = (f32[64,48,64]{2,1,0:T(8,128)S(1)}, f32[64,48,64]{2,1,0:T(8,128)}, u32[]{:S(2)}) copy-start(f32[64,48,64]{2,1,0:T(8,128)} %gather_fusion.2) | copy-start | bytes 2359300
  117.1 8.9 %copy-start.3 = (f32[48,64,64]{2,1,0:T(8,128)S(1)}, f32[48,64,64]{2,1,0:T(8,128)}, u32[]{:S(2)}) copy-start(f32[48,64,64]{2,1,0:T(8,128)} %reshape.127) | copy-start | bytes 2359300
  121.1 14.7 %collective-permute-start.3 = (f32[3,16,512]{2,1,0:T(8,128)S(1)}, f32[3,16,512]{2,1,0:T(8,128)S(1)}, u32[]{:S(2)}, u32[]{:S(2)}) collective-permute-start(f32[3,16,512]{2,1,0:T(8,128)S(1)} %reshape.130), channel_id=1, source_target_pairs={{0,4},{4,8},{8,12},{12,16},{16,20},{20,24},{24,28},{1,5},{5,9},{9,... | collective-permute-start | bytes 294920 | tf_op jit(solution)/shard_map/ppermute | solution.py:15
  133.8 2.0 %copy-start.5 = (f32[3,16,4096]{2,1,0:T(8,128)S(1)}, f32[3,16,4096]{2,1,0:T(8,128)}, u32[]{:S(2)}) copy-start(f32[3,16,4096]{2,1,0:T(8,128)} %copy-done.4) | copy-start | bytes 2359300
  133.8 22.3 %copy-start.8 = (f32[3,4096]{1,0:T(4,128)S(1)}, f32[3,4096]{1,0:T(4,128)}, u32[]{:S(2)}) copy-start(f32[3,4096]{1,0:T(4,128)} %param.21) | copy-start | bytes 147460
